TPU v7x, 32 devices: a whole 2x2x4 slice. The times are simulated.
32 devices in a mesh: blk: 16 (over z, y, x), col: 2 (over core).
Axes of the slice: x: 2, y: 2, z: 4, core: 2. Of those that a mesh axis runs over, the one named last changes fastest.
Arguments:
- queries: bfloat16 [128, 16384], P('blk', 'col'), may hold values from -6 to 6
- factor: bfloat16 [16384, 1024], P('col', 'blk'), may hold values from -0.046875 to 0.046875
- eigenvalues: float32 [1024], replicated, may hold values from 0.05 to 20
- damping: float32 [1], replicated, may hold values from 0.5 to 2
- train_rows: bfloat16 [16384, 16384], P('blk', 'col'), may hold values from -0.046875 to 0.046875
Outputs:
- scores: bfloat16 [128, 16384], P('col', 'blk')
All inputs are finite; a program needn't handle non-finite values.
Results may differ from a plain program's by a relative error of at most 0.0049.
Values may be sent and summed in bfloat16 or wider, within the bound.
A program may use at most 64 MiB of HBM per device.

v0:
```python
import jax
import jax.numpy as jnp
from jax import lax
from jax.sharding import PartitionSpec as P


def row_scores(block_rows, train_rows):
    return jnp.einsum("qk,nk->qn", block_rows, train_rows, preferred_element_type=jnp.float32)


def per_device(queries, factor, eigenvalues, damping, train_rows):
    damp_value = damping[0]
    weights = eigenvalues / (eigenvalues + damp_value)
    rank_slice = factor.shape[1]
    every_query = lax.all_gather(queries, "blk", axis=0, tiled=True)
    partial_value = jnp.dot(every_query, factor, preferred_element_type=jnp.float32)
    coefficient = lax.psum(partial_value, "col")
    slice_weights = lax.dynamic_slice_in_dim(
        weights, lax.axis_index("blk") * rank_slice, rank_slice
    )
    scaled = coefficient * slice_weights[None, :]
    correction_part = jnp.dot(scaled, factor.astype(jnp.float32).T, precision=lax.Precision.HIGHEST)
    correction = lax.psum(correction_part, "blk")
    pre_all = ((every_query.astype(jnp.float32) - correction) / damp_value).astype(jnp.bfloat16)
    partial_scores = row_scores(pre_all, train_rows)
    scores = lax.psum_scatter(partial_scores, "col", scatter_dimension=0, tiled=True)
    return scores.astype(jnp.bfloat16)


def solution(mesh):
    in_specs = (P("blk", "col"), P("col", "blk"), P(), P(), P("blk", "col"))
    out_specs = P("col", "blk")
    return jax.shard_map(
        per_device, mesh=mesh, in_specs=in_specs, out_specs=out_specs, check_vma=False
    )
```

profile of v0, /device:TPU:0, one launch (start us, length us, event | category | flops | bytes accessed | tf_op | source)
XLA Modules:
  0.0 279.0 jit_solution(8576192515819052841)
XLA Ops:
  6.5 0.0 copy-start
  6.5 0.0 all-gather.2.cloned.1.call-start
  6.5 0.7 all-gather.2.cloned.1.call-update
  7.3 0.0 all-reduce.2.cloned.1.call-start
  8.0 0.7 add_divide_fusion
  8.6 0.1 dynamic_slice.3
  8.7 64.5 %all-gather.2.cloned.1.call-done = bf16[128,8192]{1,0:T(8,128)(2,1)} async-done(((bf16[8,8192]{1,0:T(8,128)(2,1)}), bf16[128,8192]{1,0:T(8,128)(2,1)}) %all-gather.2.cloned.1.call-update) | async-done | bytes 2097168 | tf_op jit(solution)/shard_map/all_gather | solution.py:15
  73.2 0.0 copy-done
  73.2 2.3 fusion.5
  75.5 3.6 %psum.14 = f32[128,64]{1,0:T(8,128)S(1)} all-reduce(f32[128,64]{1,0:T(8,128)S(1)} %fusion.5), channel_id=1, replica_groups=mesh['blk'=16,'col'=2] {'col'}, use_global_device_ids=true, to_apply=%region_0.0 | all-reduce | flops 8192 | bytes 65536 | tf_op jit(solution)/shard_map/psum | solution.py:17
  79.1 0.0 copy-start.1
  79.1 3.7 %fusion.2 = f32[128,8192]{1,0:T(8,128)} fusion(bf16[8192,64]{0,1:T(8,128)(2,1)S(1)} %copy-done, f32[128,64]{1,0:T(8,128)S(1)} %psum.14, f32[64]{0:T(128)S(1)} %dynamic_slice.3), kind=kOutput, calls=%fused_computation.3 | convolution fusion | flops 805314560 | bytes 5275904 | tf_op jit(solution)/shard_map/dot_general | solution.py:22
  82.9 0.0 all-reduce.2.cloned.1.call-update
  82.9 0.0 reduce-scatter.2.cloned.1.call-start
  83.0 167.2 %all-reduce.2.cloned.1.call-done = f32[128,8192]{1,0:T(8,128)} async-done(((f32[128,8192]{1,0:T(8,128)}), f32[128,8192]{1,0:T(8,128)}) %all-reduce.2.cloned.1.call-update) | async-done | bytes 4194320 | tf_op jit(solution)/shard_map/psum | solution.py:23
  250.2 0.0 copy-done.1
  250.2 13.5 %fusion = f32[128,1024]{1,0:T(8,128)} fusion(bf16[1024,8192]{1,0:T(8,128)(2,1)} %param.9, f32[128,8192]{1,0:T(8,128)} %all-reduce.2.cloned.1.call-done, bf16[128,8192]{1,0:T(8,128)(2,1)S(1)} %copy-done.1, f32[]{:T(128)} %bitcast.6), kind=kOutput, calls=%fused_computation.1 | convolution fusion | flops 2151677952 | bytes 23592964 | tf_op jit(solution)/shard_map/qk,nk->qn/dot_general | solution.py:8
  263.7 0.0 reduce-scatter.2.cloned.1.call-update
  263.7 7.1 %reduce-scatter.2.cloned.1.call-done = f32[64,1024]{1,0:T(8,128)} async-done(((f32[128,1024]{1,0:T(8,128)}), f32[64,1024]{1,0:T(8,128)}) %reduce-scatter.2.cloned.1.call-update) | async-done | bytes 262160 | tf_op jit(solution)/shard_map/reduce_scatter | solution.py:26
  270.8 1.6 convert_element_type.12
Async XLA Ops:
  6.5 66.7 %copy-start = (bf16[8192,64]{0,1:T(8,128)(2,1)S(1)}, bf16[8192,64]{0,1:T(8,128)(2,1)}, u32[]{:S(2)}) copy-start(bf16[8192,64]{0,1:T(8,128)(2,1)} %param.6) | copy-start | bytes 3145732
  6.5 66.7 %all-gather.2.cloned.1.call-start = ((), (), s32[]{:S(2)}) async-start(), calls=%async_computation.1 | async-start | bytes 2228224 | tf_op jit(solution)/shard_map/all_gather | solution.py:15
  7.3 242.9 %all-reduce.2.cloned.1.call-start = ((), (), s32[]{:S(2)}) async-start(), calls=%async_computation.2 | async-start | bytes 8388608 | tf_op jit(solution)/shard_map/psum | solution.py:23
  79.1 171.0 %copy-start.1 = (bf16[128,8192]{1,0:T(8,128)(2,1)S(1)}, bf16[128,8192]{1,0:T(8,128)(2,1)}, u32[]{:S(2)}) copy-start(bf16[128,8192]{1,0:T(8,128)(2,1)} %all-gather.2.cloned.1.call-done) | copy-start | bytes 6291460
  82.9 187.9 %reduce-scatter.2.cloned.1.call-start = ((), (), s32[]{:S(2)}) async-start(), calls=%async_computation.3 | async-start | bytes 786432 | tf_op jit(solution)/shard_map/reduce_scatter | solution.py:26
Sparse Core Ops, SparseCore 0:
  10.1 63.0 all-gather.1
  83.0 167.0 all-reduce.1
  263.8 6.9 reduce-scatter.1
where the time goes:
time: 279 us
  waiting for transfers between devices  240 us (86%)
  matrix products  19.5 us (7%)
  between operations  13.8 us (5%)
  blocking collectives  3.59 us (1%)
    psum x1, waiting for transfers between devices, per_device(): correction = lax.psum(correction_part, 'blk')  167 us
    all_gather x1, waiting for transfers between devices, per_device(): every_query = lax.all_gather(queries, 'blk', axis=0, tiled=True)  64.5 us
    dot_general x1, matrix products, row_scores(): jnp.einsum('qk,nk->qn', block_rows, train_rows, preferred_element_type=jn...  13.5 us
    reduce_scatter x1, waiting for transfers between devices, per_device(): lax.psum_scatter(partial_scores, 'col', scatter_dimension=0, tiled=True)  7.13 us
  transfers between devices with their start and end apart: 3, of which 3 were waited for; matrix products, arithmetic and copies ran while one was open for 0% of the time, Pallas kernels for 0%

commit v1 on v0

--- a/solution.py
+++ b/solution.py
@@ -20,7 +20,11 @@
     )
     scaled = coefficient * slice_weights[None, :]
     correction_part = jnp.dot(scaled, factor.astype(jnp.float32).T, precision=lax.Precision.HIGHEST)
-    correction = lax.psum(correction_part, "blk")
+    correction = correction_part
+    for hop in (1, 2, 4, 8):
+        correction = correction + lax.ppermute(
+            correction, "blk", [(dev, dev ^ hop) for dev in range(16)]
+        )
     pre_all = ((every_query.astype(jnp.float32) - correction) / damp_value).astype(jnp.bfloat16)
     partial_scores = row_scores(pre_all, train_rows)
     scores = lax.psum_scatter(partial_scores, "col", scatter_dimension=0, tiled=True)

time: 279 us -> 569 us (2.04)
  waiting for transfers between devices: 240 us -> 523 us
  starting transfers between devices: 0.08 us -> 6.16 us
    ppermute x0 -> x4, waiting for transfers between devices: none -> 451 us  [per_device(): lax.ppermute(correction, 'blk', [(dev, dev ^ hop) for dev in range(16)])]
    psum x1 -> x0, waiting for transfers between devices: 167 us -> none  [per_device(): correction = lax.psum(correction_part, 'blk')]
    ppermute x0 -> x4, starting transfers between devices: none -> 6.12 us  [per_device(): lax.ppermute(correction, 'blk', [(dev, dev ^ hop) for dev in range(16)])]
  transfers between devices with their start and end apart: 3 -> 6, of which waited for: 3 -> 6; matrix products, arithmetic and copies ran while one was open for 0% -> 0% of each run, Pallas kernels for 0% -> 0%
where the time goes in v1:
time: 569 us; the launch traced here: 568 us
  waiting for transfers between devices  523 us (92%)
  matrix products  15.5 us (3%)
  between operations  14.1 us (2%)
  starting transfers between devices  6.16 us (1%)
    ppermute x4, waiting for transfers between devices, per_device(): lax.ppermute(correction, 'blk', [(dev, dev ^ hop) for dev in range(16)])  451 us
    all_gather x1, waiting for transfers between devices, per_device(): every_query = lax.all_gather(queries, 'blk', axis=0, tiled=True)  64.5 us
    dot_general x1, matrix products, row_scores(): jnp.einsum('qk,nk->qn', block_rows, train_rows, preferred_element_type=jn...  11.4 us
  transfers between devices with their start and end apart: 6, of which 6 were waited for; matrix products, arithmetic and copies ran while one was open for 0% of the time, Pallas kernels for 0%

profile of v1, /device:TPU:0, one launch (start us, length us, event | category | flops | bytes accessed | tf_op | source)
XLA Modules:
  0.0 568.4 jit_solution(12359450322443537457)
XLA Ops:
  6.5 0.7 all-gather.2.cloned.1.call-update
  7.3 0.0 reduce-scatter.2.cloned.1.call-start
  8.0 0.7 add_divide_fusion
  8.6 0.1 dynamic_slice.3
  8.7 64.5 %all-gather.2.cloned.1.call-done = bf16[128,8192]{1,0:T(8,128)(2,1)} async-done(((bf16[8,8192]{1,0:T(8,128)(2,1)}), bf16[128,8192]{1,0:T(8,128)(2,1)}) %all-gather.2.cloned.1.call-update) | async-done | bytes 2097168 | tf_op jit(solution)/shard_map/all_gather | solution.py:15
  73.2 2.3 fusion.5
  75.5 3.6 psum.7
  79.1 1.8 fusion.2
  80.9 1.3 collective-permute-start
  82.3 91.5 %collective-permute-done = f32[128,8192]{1,0:T(8,128)S(1)} collective-permute-done((f32[128,8192]{1,0:T(8,128)S(1)}, f32[128,8192]{1,0:T(8,128)S(1)}, u32[]{:S(2)}, u32[]{:S(2)}) %collective-permute-start) | collective-permute-done | bytes 4194336 | tf_op jit(solution)/shard_map/ppermute | solution.py:25
  173.8 0.5 add.28
  174.3 1.5 collective-permute-start.1
  175.9 90.5 %collective-permute-done.1 = f32[128,8192]{1,0:T(8,128)S(1)} collective-permute-done((f32[128,8192]{1,0:T(8,128)S(1)}, f32[128,8192]{1,0:T(8,128)S(1)}, u32[]{:S(2)}, u32[]{:S(2)}) %collective-permute-start.1) | collective-permute-done | bytes 4194336 | tf_op jit(solution)/shard_map/ppermute | solution.py:25
  266.3 0.5 add.29
  266.9 1.5 collective-permute-start.2
  268.4 89.6 %collective-permute-done.2 = f32[128,8192]{1,0:T(8,128)S(1)} collective-permute-done((f32[128,8192]{1,0:T(8,128)S(1)}, f32[128,8192]{1,0:T(8,128)S(1)}, u32[]{:S(2)}, u32[]{:S(2)}) %collective-permute-start.2) | collective-permute-done | bytes 4194336 | tf_op jit(solution)/shard_map/ppermute | solution.py:25
  358.0 0.5 add.30
  358.6 1.7 collective-permute-start.3
  360.3 179.4 %collective-permute-done.3 = f32[128,8192]{1,0:T(8,128)S(1)} collective-permute-done((f32[128,8192]{1,0:T(8,128)S(1)}, f32[128,8192]{1,0:T(8,128)S(1)}, u32[]{:S(2)}, u32[]{:S(2)}) %collective-permute-start.3) | collective-permute-done | bytes 4194336 | tf_op jit(solution)/shard_map/ppermute | solution.py:25
  539.7 1.9 copy-done.2
  541.6 11.4 %fusion = f32[128,1024]{1,0:T(8,128)} fusion(bf16[1024,8192]{1,0:T(8,128)(2,1)} %param.9, f32[128,8192]{1,0:T(8,128)S(1)} %add.30, f32[128,8192]{1,0:T(8,128)} %copy-done.2, bf16[128,8192]{1,0:T(8,128)(2,1)S(1)} %copy-done.1, f32[]{:T(128)} %bitcast.6), kind=kOutput, calls=%fused_computation.1 | convolution fusion | flops 2152726528 | bytes 27787268 | tf_op jit(solution)/shard_map/qk,nk->qn/dot_general | solution.py:8
  553.0 0.0 reduce-scatter.2.cloned.1.call-update
  553.1 6.9 %reduce-scatter.2.cloned.1.call-done = f32[64,1024]{1,0:T(8,128)} async-done(((f32[128,1024]{1,0:T(8,128)}), f32[64,1024]{1,0:T(8,128)}) %reduce-scatter.2.cloned.1.call-update) | async-done | bytes 262160 | tf_op jit(solution)/shard_map/reduce_scatter | solution.py:30
  559.9 1.6 convert_element_type.12
  (6 shorter events, 0.0 us)
Async XLA Ops:
  6.5 66.7 %copy-start = (bf16[8192,64]{0,1:T(8,128)(2,1)S(1)}, bf16[8192,64]{0,1:T(8,128)(2,1)}, u32[]{:S(2)}) copy-start(bf16[8192,64]{0,1:T(8,128)(2,1)} %param.6) | copy-start | bytes 3145732
  6.5 66.7 %all-gather.2.cloned.1.call-start = ((), (), s32[]{:S(2)}) async-start(), calls=%async_computation.1 | async-start | bytes 2228224 | tf_op jit(solution)/shard_map/all_gather | solution.py:15
  7.3 552.7 %reduce-scatter.2.cloned.1.call-start = ((), (), s32[]{:S(2)}) async-start(), calls=%async_computation.2 | async-start | bytes 786432 | tf_op jit(solution)/shard_map/reduce_scatter | solution.py:30
  80.9 92.9 %collective-permute-start = (f32[128,8192]{1,0:T(8,128)S(1)}, f32[128,8192]{1,0:T(8,128)S(1)}, u32[]{:S(2)}, u32[]{:S(2)}) collective-permute-start(f32[128,8192]{1,0:T(8,128)S(1)} %fusion.2), channel_id=1, source_target_pairs={{0,2},{2,0},{4,6},{6,4},{8,10},{10,8},{12,14},{14,12},{16,18},{18,... | collective-permute-start | bytes 12582920 | tf_op jit(solution)/shard_map/ppermute | solution.py:25
  174.3 92.0 %collective-permute-start.1 = (f32[128,8192]{1,0:T(8,128)S(1)}, f32[128,8192]{1,0:T(8,128)S(1)}, u32[]{:S(2)}, u32[]{:S(2)}) collective-permute-start(f32[128,8192]{1,0:T(8,128)S(1)} %add.28), channel_id=1, source_target_pairs={{0,4},{2,6},{4,0},{6,2},{8,12},{10,14},{12,8},{14,10},{16,20},{18,... | collective-permute-start | bytes 12582920 | tf_op jit(solution)/shard_map/ppermute | solution.py:25
  266.9 274.8 %copy-start.1 = (bf16[128,8192]{1,0:T(8,128)(2,1)S(1)}, bf16[128,8192]{1,0:T(8,128)(2,1)}, u32[]{:S(2)}) copy-start(bf16[128,8192]{1,0:T(8,128)(2,1)} %all-gather.2.cloned.1.call-done) | copy-start | bytes 6291460
  266.9 91.2 %collective-permute-start.2 = (f32[128,8192]{1,0:T(8,128)S(1)}, f32[128,8192]{1,0:T(8,128)S(1)}, u32[]{:S(2)}, u32[]{:S(2)}) collective-permute-start(f32[128,8192]{1,0:T(8,128)S(1)} %add.29), channel_id=1, source_target_pairs={{0,8},{2,10},{4,12},{6,14},{8,0},{10,2},{12,4},{14,6},{16,24},{18,... | collective-permute-start | bytes 12582920 | tf_op jit(solution)/shard_map/ppermute | solution.py:25
  358.6 181.1 %collective-permute-start.3 = (f32[128,8192]{1,0:T(8,128)S(1)}, f32[128,8192]{1,0:T(8,128)S(1)}, u32[]{:S(2)}, u32[]{:S(2)}) collective-permute-start(f32[128,8192]{1,0:T(8,128)S(1)} %add.30), channel_id=1, source_target_pairs={{0,16},{2,18},{4,20},{6,22},{8,24},{10,26},{12,28},{14,30},{16,0},... | collective-permute-start | bytes 12582920 | tf_op jit(solution)/shard_map/ppermute | solution.py:25
  539.7 1.9 copy-start.2
Sparse Core Ops, SparseCore 0:
  10.1 63.0 all-gather.1
  553.2 6.7 reduce-scatter.1
